TPU v7x, 32 devices: a whole 2x2x4 slice. The times are simulated.
32 devices in a mesh: groups: 2 (over y), rank: 16 (over z, x, core).
Axes of the slice: x: 2, y: 2, z: 4, core: 2. Of those that a mesh axis runs over, the one named last changes fastest.
Arguments:
- pool: bfloat16 [512, 1024], P(('groups', 'rank')), parts along dimension 0, may hold values from -6 to 6
- kv_cache: bfloat16 [128, 4, 64, 256], P(('groups', 'rank')), parts along dimension 0
- w_qu: bfloat16 [1024, 1024], replicated, may hold values from -0.1875 to 0.1875
- w_out: bfloat16 [512, 1024], replicated, may hold values from -0.25 to 0.25
- norm_gain: float32 [512], replicated, may hold values from 0.1 to 1.9
- cand_ids: int32 [8, 2048], P('groups'), parts along dimension 0, may hold values from 0 to 255
- ranker: int32 [4], replicated, may hold values from 0 to 3, each once
- hist_blocks: int32 [8], P('groups'), parts along dimension 0, may hold values from 4 to 16, as said below
- cache_slot: int32 [8, 16], P('groups'), parts along dimension 0, may hold values from 0 to 63, as said below
Outputs:
- ranked: bfloat16 [16384, 1024], P(('groups', 'rank')), parts along dimension 0
There are 2 independent parts, one for each index of `groups`. A program takes and returns all parts, laid end to end along the dimension named above; an argument that names none is the same for every part. Nothing has to cross between parts.
Inputs may be any that keep to these rules, and one draw needn't show every extreme that they name: Block b of user u (b < 16) is held in slot cache_slot[u, b], which lies on device cache_slot[u, b] // 4 of the rank axis. Each slot holds exactly one pair (u, b); the 16 blocks of one user lie on 16 different devices. `ranker`: each ranking group scores exactly one user. User u's history is its blocks 0 to hist_blocks[u] - 1; its other blocks are unused. Some user has 16 blocks.
All inputs are finite; a program needn't handle non-finite values.
Results may differ from a plain program's by a relative error of at most 0.0054.
Values may be sent and summed in bfloat16 or wider, within the bound.
No kernel may reach another device: no remote copies, remote signals or barrier semaphores. Data moves between devices by JAX's collectives and lax.ppermute only.
A program may use at most 128 MiB of HBM per device.

v0:
```python
import functools
import math

import jax
import jax.numpy as jnp
from jax import lax
from jax.experimental import pallas as pl
from jax.experimental.pallas import tpu as pltpu
from jax.sharding import PartitionSpec as P


norm_eps = 1e-05
VMEM = pl.BlockSpec(memory_space=pltpu.VMEM)
SMEM = pl.BlockSpec(memory_space=pltpu.SMEM)
HBM = pl.BlockSpec(memory_space=pltpu.HBM)


def in_hbm(array):
    return pltpu.with_memory_space_constraint(array, pltpu.HBM)


def swap_with(shard, mask):
    return lax.ppermute(shard, "rank", [(i, i ^ mask) for i in range(lax.axis_size("rank"))])


def call(kernel, out_shape, in_specs, scratch=(), flops=0, bytes_accessed=0):
    single = not isinstance(out_shape, (list, tuple))
    return pl.pallas_call(
        kernel,
        out_shape=out_shape,
        in_specs=in_specs,
        out_specs=VMEM if single else [VMEM] * len(out_shape),
        scratch_shapes=list(scratch),
        compiler_params=pltpu.CompilerParams(vmem_limit_bytes=48 * 1024 * 1024),
        cost_estimate=pl.CostEstimate(flops=flops, bytes_accessed=bytes_accessed, transcendentals=0),
    )


def pick_kernel(groups, size, me_ref, ranker_ref, length_ref, slot_ref, kv_ref, *refs):
    outs, (ranker, length, slots, sem) = refs[:groups], refs[groups:]
    slots_here = kv_ref.shape[0]
    users, blocks = slots.shape
    loads = [
        pltpu.make_async_copy(ref, to, sem.at[i])
        for i, (ref, to) in enumerate(((ranker_ref, ranker), (length_ref, length), (slot_ref, slots)))
    ]
    for load in loads:
        load.start()
    for load in loads:
        load.wait()
    first = me_ref[0] * slots_here
    my_group = me_ref[0] // size

    def held_by(user):
        def step(b, found):
            local = slots[user, b] - first
            here = (local >= 0) & (local < slots_here)
            return jnp.where(here, local, found[0]), jnp.where(here, b, found[1])

        return lax.fori_loop(0, blocks, step, (0, 0), unroll=blocks <= 16)

    def user_of(group):
        def step(u, found):
            return jnp.where(ranker[u] == group, u, found)

        return lax.fori_loop(0, users, step, 0, unroll=users <= 16)

    lives = []
    for k in range(groups):
        user = user_of(my_group ^ k)
        slot, at = held_by(user)
        lives.append(at < length[user])

        @pl.when(lives[k])
        def _(k=k, slot=slot):
            pltpu.make_async_copy(kv_ref.at[slot], outs[k], sem.at[3 + k]).start()

        @pl.when(jnp.logical_not(lives[k]))
        def _(k=k):
            outs[k][...] = jnp.zeros_like(outs[k])

    for k in range(groups):

        @pl.when(lives[k])
        def _(k=k):
            pltpu.make_async_copy(kv_ref.at[0], outs[k], sem.at[3 + k]).wait()


def project(heads, rows_ref, w_ref, q_ref, gate_ref):
    dim = w_ref.shape[1] // (2 * heads)
    qu = jax.nn.silu(jnp.dot(rows_ref[...], w_ref[...], preferred_element_type=jnp.float32))
    qu = qu.astype(jnp.bfloat16)
    for h in range(heads):
        cols = slice(h * dim, (h + 1) * dim)
        q_ref[:, cols] = qu[:, 2 * h * dim : (2 * h + 1) * dim]
        gate_ref[:, cols] = qu[:, (2 * h + 1) * dim : (2 * h + 2) * dim]


def project_kernel(heads, rows_ref, w_ref, q_ref, gate_ref):
    project(heads, rows_ref, w_ref, q_ref, gate_ref)


def project_and_place_kernel(
    heads, size, pool_here, me_ref, rows_ref, w_ref, ranker_ref, ids_ref, q_ref, gate_ref, hot_ref, ranker, ids, sem
):
    users = ids_ref.shape[0]
    share = ids.shape[1]
    me = me_ref[0]
    my_group, my_place = me // size, me % size
    loads = (
        pltpu.make_async_copy(ranker_ref, ranker, sem.at[0]),
        pltpu.make_async_copy(ids_ref.at[:, pl.ds(pl.multiple_of(my_place * share, share), share)], ids, sem.at[1]),
    )
    for load in loads:
        load.start()
    project(heads, rows_ref, w_ref, q_ref, gate_ref)
    for load in loads:
        load.wait()

    def step(u, found):
        return jnp.where(ranker[u] == my_group, u, found)

    my_user = lax.fori_loop(0, users, step, 0, unroll=users <= 16)
    item = ids[pl.ds(my_user, 1), :]
    owner = item // pool_here
    differs = (owner % size) ^ my_place
    rows = hot_ref.shape[1] // 2
    place = (differs % 2) * rows + (differs // 2) * (rows // 2)
    place = place + ((owner // size) ^ my_group) * pool_here + item % pool_here
    part = math.gcd(2 * rows, 256)
    for first in range(0, 2 * rows, part):
        at = lax.broadcasted_iota(jnp.int32, (part, share), 0) + first
        hot = jnp.where(at == place, 1.0, 0.0)
        hot_ref[:, first : first + part] = jnp.transpose(hot).astype(jnp.bfloat16)


def attend_kernel(scale, q_own_ref, q_far_ref, *refs):
    kv, sum_ref, sent_ref = refs[:-2], refs[-2], refs[-1]
    heads, _, pair = kv[0].shape
    dim = pair // 2
    half = q_own_ref.shape[0]
    tile = math.gcd(half, 64)
    together = math.gcd(len(kv), 4)

    def one_tile(t, _):
        at = pl.ds(pl.multiple_of(t * tile, tile), tile)
        low = pl.ds(pl.multiple_of(t * tile + half, tile), tile)
        for h in range(heads):
            cols = slice(h * dim, (h + 1) * dim)
            query = jnp.concatenate([q_own_ref[at, cols], q_far_ref[at, cols]], axis=0)
            total = None
            for first in range(0, len(kv), together):
                parts = [kv[k][h] for k in range(first, first + together)]
                keys = jnp.concatenate([p[:, :dim] for p in parts], axis=0)
                values = jnp.concatenate([p[:, dim:] for p in parts], axis=0)
                scores = lax.dot_general(
                    query, keys, (((1,), (1,)), ((), ())), preferred_element_type=jnp.float32
                )
                weights = jax.nn.silu(scores * scale).astype(jnp.bfloat16)
                add = jnp.dot(weights, values, preferred_element_type=jnp.float32)
                total = add if total is None else total + add
            sum_ref[at, cols] = total[:tile]
            sum_ref[low, cols] = total[tile:]
            sent_ref[at, cols] = total[:tile].astype(jnp.bfloat16)
            sent_ref[low, cols] = total[tile:].astype(jnp.bfloat16)
        return 0

    lax.fori_loop(0, half // tile, one_tile, 0, unroll=half == tile)


def finish_kernel(sum_ref, sent_ref, gate_own_ref, gate_far_ref, own_ref, far_ref, gain_ref, w_ref, out_ref):
    half = own_ref.shape[0]
    tile = math.gcd(half, 64)
    for side, rows, gates in ((0, own_ref, gate_own_ref), (1, far_ref, gate_far_ref)):
        for first in range(0, half, tile):
            mine = slice(side * half + first, side * half + first + tile)
            theirs = slice((1 - side) * half + first, (1 - side) * half + first + tile)
            here = slice(first, first + tile)
            attended = sum_ref[mine, :] + sent_ref[theirs, :].astype(jnp.float32)
            mean = jnp.mean(attended, axis=1, keepdims=True)
            variance = jnp.mean(attended * attended, axis=1, keepdims=True) - mean * mean
            hidden = (attended - mean) * lax.rsqrt(variance + norm_eps) * gain_ref[...]
            hidden = (hidden * gates[here, :].astype(jnp.float32)).astype(jnp.bfloat16)
            mixed = jnp.dot(hidden, w_ref[...], preferred_element_type=jnp.float32)
            mixed = mixed + rows[here, :].astype(jnp.float32)
            out_ref[mine, :] = mixed.astype(jnp.bfloat16)


def select_kernel(hot_ref, own_ref, far_ref, out_ref, buffer, sem):
    rows = own_ref.shape[0]
    share = hot_ref.shape[0]
    tile = math.gcd(share, 128)
    copies = []
    for i, first in enumerate(range(0, share, tile)):
        at = slice(first, first + tile)
        picked = jnp.dot(hot_ref[at, :rows], own_ref[...], preferred_element_type=jnp.float32)
        picked = picked + jnp.dot(hot_ref[at, rows:], far_ref[...], preferred_element_type=jnp.float32)
        buffer[at, :] = picked.astype(jnp.bfloat16)
        copies.append(pltpu.make_async_copy(buffer.at[at], out_ref.at[at], sem.at[i]))
        copies[-1].start()
    for copy in copies:
        copy.wait()


def layer(pool, kv_cache, w_qu, w_out, norm_gain, cand_ids, ranker, hist_blocks, cache_slot):
    devices = lax.axis_size("rank")
    me = lax.axis_index("rank").astype(jnp.int32).reshape(1)
    _, heads, block, pair = kv_cache.shape
    dim = pair // 2
    users, _ = cache_slot.shape
    pool_here, width = pool.shape
    groups = users
    size = devices // groups
    assert size == 4 and groups & (groups - 1) == 0
    shape = jax.ShapeDtypeStruct
    dma = pltpu.SemaphoreType.DMA

    picked = call(
        functools.partial(pick_kernel, groups, size),
        [shape((heads, block, pair), jnp.bfloat16)] * groups,
        [SMEM, HBM, HBM, HBM, HBM],
        [
            pltpu.SMEM(ranker.shape, jnp.int32),
            pltpu.SMEM(hist_blocks.shape, jnp.int32),
            pltpu.SMEM(cache_slot.shape, jnp.int32),
            dma((3 + groups,)),
        ],
        bytes_accessed=2 * kv_cache.size * 2,
    )(me, *[in_hbm(a) for a in (ranker, hist_blocks, cache_slot, kv_cache)])
    column, kv = [pool], [picked[0]]
    for k in range(1, groups):
        column.append(swap_with(pool, size * k))
        kv.append(swap_with(picked[k], size * k))

    own_rows = jnp.concatenate(column, axis=0)
    far_rows = swap_with(own_rows, 2)
    half = own_rows.shape[0]
    rows = 2 * half
    share = cand_ids.shape[1] // size
    cost = dict(flops=2 * half * width * w_qu.shape[1], bytes_accessed=half * width * 4)
    halves = [shape((half, heads * dim), jnp.bfloat16)] * 2
    q_own, gate_own, hot = call(
        functools.partial(project_and_place_kernel, heads, size, pool_here),
        halves + [shape((share, 2 * rows), jnp.bfloat16)],
        [SMEM, VMEM, VMEM, HBM, HBM],
        [pltpu.SMEM(ranker.shape, jnp.int32), pltpu.VMEM((users, share), jnp.int32), dma((2,))],
        **cost,
    )(me, own_rows, w_qu, in_hbm(ranker), in_hbm(cand_ids))
    q_far, gate_far = call(functools.partial(project_kernel, heads), halves, [VMEM] * 2, **cost)(far_rows, w_qu)

    for k in range(groups):
        after = q_own if k < 2 else q_far
        ready, after = lax.optimization_barrier((kv[k], after))
        if k < 2:
            q_own = after
        else:
            q_far = after
        kv.append(swap_with(ready, 1))
    sums, sent = call(
        functools.partial(attend_kernel, 1.0 / math.sqrt(dim)),
        [shape((rows, heads * dim), jnp.float32), shape((rows, heads * dim), jnp.bfloat16)],
        [VMEM] * (2 + len(kv)),
        flops=4 * rows * len(kv) * block * heads * dim,
        bytes_accessed=len(kv) * heads * block * pair * 2,
    )(q_own, q_far, *kv)
    sent = swap_with(sent, 2)
    table = call(
        finish_kernel,
        shape((rows, width), jnp.bfloat16),
        [VMEM] * 8,
        flops=2 * rows * heads * dim * width,
        bytes_accessed=w_out.size * 2,
    )(sums, sent, gate_own, gate_far, own_rows, far_rows, norm_gain[None, :], w_out)
    table_far = swap_with(table, 1)
    return pl.pallas_call(
        select_kernel,
        out_shape=shape((share, width), jnp.bfloat16),
        in_specs=[VMEM] * 3,
        out_specs=HBM,
        scratch_shapes=[pltpu.VMEM((share, width), jnp.bfloat16), dma((share // math.gcd(share, 128),))],
        compiler_params=pltpu.CompilerParams(vmem_limit_bytes=48 * 1024 * 1024),
        cost_estimate=pl.CostEstimate(
            flops=2 * share * 2 * rows * width, bytes_accessed=share * width * 2, transcendentals=0
        ),
        name="select",
    )(hot, table, table_far)


def solution(mesh):
    in_specs = (
        P(("groups", "rank"), None),
        P(("groups", "rank"), None, None, None),
        P(),
        P(),
        P(),
        P("groups", None),
        P(),
        P("groups"),
        P("groups", None),
    )
    out_specs = P(("groups", "rank"), None)
    return jax.shard_map(layer, mesh=mesh, in_specs=in_specs, out_specs=out_specs, check_vma=False)
```

profile of v0, /device:TPU:0, one launch (start us, length us, event | category | flops | bytes accessed | tf_op | source)
XLA Modules:
  0.0 35.0 jit_solution(17128942245331537093)
XLA Ops:
  0.0 4.1 %collective-permute-start.1 = (bf16[16,1024]{1,0:T(8,128)(2,1)}, bf16[16,1024]{1,0:T(8,128)(2,1)S(1)}, u32[]{:S(2)}, u32[]{:S(2)}) collective-permute-start(bf16[16,1024]{1,0:T(8,128)(2,1)} %param.9), channel_id=1, source_target_pairs={{0,8},{1,9},{2,10},{3,11},{4,12},{5,13},{6,14},{7,15},{8,0},{9,1},... | collective-permute-start | bytes 98312 | tf_op jit(solution)/shard_map/ppermute | solution.py:23
  4.1 1.6 %collective-permute-start = (bf16[16,1024]{1,0:T(8,128)(2,1)}, bf16[16,1024]{1,0:T(8,128)(2,1)S(1)}, u32[]{:S(2)}, u32[]{:S(2)}) collective-permute-start(bf16[16,1024]{1,0:T(8,128)(2,1)} %param.9), channel_id=1, source_target_pairs={{0,4},{1,5},{2,6},{3,7},{4,0},{5,1},{6,2},{7,3},{8,12},{9,13},{10,... | collective-permute-start | bytes 98312 | tf_op jit(solution)/shard_map/ppermute | solution.py:23
  5.6 1.8 %shard_map.92 = (bf16[4,64,256]{2,1,0:T(8,128)(2,1)S(1)}, bf16[4,64,256]{2,1,0:T(8,128)(2,1)S(1)}, bf16[4,64,256]{2,1,0:T(8,128)(2,1)S(1)}, bf16[4,64,256]{2,1,0:T(8,128)(2,1)S(1)}) custom-call(s32[1]{0:T(128)} %bitcast.me_ref, s32[4]{0:T(128)} %ranker_ref.3, s32[4]{0:T(128)} %length_ref.1, s32[4,16]{1,0:T(4,128)} %slot_ref.1, bf16[4,4,64,256]{3,2,1,0:T(8,128)(2,1)} %kv_ref.1), custom_call_target="tpu_custom_call" | custom-call | bytes 1048576 | tf_op jit(solution)/shard_map/pallas_call | solution.py:218
  7.5 0.9 %collective-permute-start.3 = (bf16[4,64,256]{2,1,0:T(8,128)(2,1)S(1)}, bf16[4,64,256]{2,1,0:T(8,128)(2,1)S(1)}, u32[]{:S(2)}, u32[]{:S(2)}) collective-permute-start(bf16[4,64,256]{2,1,0:T(8,128)(2,1)S(1)} %get-tuple-element.25), channel_id=1, source_target_pairs={{0,4},{1,5},{2,6},{3,7},{4,0},{5,1},{6,2},{7,3},{8,12},{9,13},{10,... | collective-permute-start | bytes 393224 | tf_op jit(solution)/shard_map/ppermute | solution.py:23
  8.4 0.8 %constant_dynamic-update-slice_fusion.3 = bf16[64,1024]{1,0:T(8,128)(2,1)S(1)} fusion(bf16[16,1024]{1,0:T(8,128)(2,1)} %param.9), kind=kLoop, calls=%fused_computation.3 | loop fusion | bytes 65536
  9.2 2.6 %collective-permute-done.2 = bf16[16,1024]{1,0:T(8,128)(2,1)S(1)} collective-permute-done((bf16[16,1024]{1,0:T(8,128)(2,1)}, bf16[16,1024]{1,0:T(8,128)(2,1)S(1)}, u32[]{:S(2)}, u32[]{:S(2)}) %collective-permute-start.2) | collective-permute-done | bytes 32800 | tf_op jit(solution)/shard_map/ppermute | solution.py:23
  11.9 1.6 %collective-permute-start.6 = (bf16[64,1024]{1,0:T(8,128)(2,1)S(1)}, bf16[64,1024]{1,0:T(8,128)(2,1)S(1)}, u32[]{:S(2)}, u32[]{:S(2)}) collective-permute-start(bf16[64,1024]{1,0:T(8,128)(2,1)S(1)} %constant_dynamic-update-slice_fusion.rows_ref.own_ref), channel_id=1, source_target_pairs={{0,2},{1,3},{2,0},{3,1},{4,6},{5,7},{6,4},{7,5},{8,10},{9,11},{10,... | collective-permute-start | bytes 393224 | tf_op jit(solution)/shard_map/ppermute | solution.py:23
  13.4 0.9 %collective-permute-start.5 = (bf16[4,64,256]{2,1,0:T(8,128)(2,1)S(1)}, bf16[4,64,256]{2,1,0:T(8,128)(2,1)S(1)}, u32[]{:S(2)}, u32[]{:S(2)}) collective-permute-start(bf16[4,64,256]{2,1,0:T(8,128)(2,1)S(1)} %get-tuple-element.31), channel_id=1, source_target_pairs={{0,8},{1,9},{2,10},{3,11},{4,12},{5,13},{6,14},{7,15},{8,0},{9,1},... | collective-permute-start | bytes 393224 | tf_op jit(solution)/shard_map/ppermute | solution.py:23
  14.3 0.3 collective-permute-start.4
  14.6 1.6 %copy-done = bf16[1024,1024]{1,0:T(8,128)(2,1)S(1)} copy-done((bf16[1024,1024]{1,0:T(8,128)(2,1)S(1)}, bf16[1024,1024]{1,0:T(8,128)(2,1)}, u32[]{:S(2)}) %copy-start) | copy-done | bytes 2097176
  16.2 1.4 %shard_map.91 = (bf16[64,512]{1,0:T(8,128)(2,1)S(1)}, bf16[64,512]{1,0:T(8,128)(2,1)S(1)}, bf16[512,256]{1,0:T(8,128)(2,1)S(1)}) custom-call(s32[1]{0:T(128)} %bitcast.me_ref, bf16[64,1024]{1,0:T(8,128)(2,1)S(1)} %constant_dynamic-update-slice_fusion.rows_ref.own_ref, bf16[1024,1024]{1,0:T(8,128)(2,1)S(1)} %copy-done, s32[4]{0:T(128)} %ranker_ref.3, ...), custom_call_target="tpu_custom_call" | custom-call | flops 134217728 | bytes 262144 | tf_op jit(solution)/shard_map/pallas_call | solution.py:242
  17.6 0.1 collective-permute-start.7
  17.7 0.5 %collective-permute-start.8 = (bf16[4,64,256]{2,1,0:T(8,128)(2,1)S(1)}, bf16[4,64,256]{2,1,0:T(8,128)(2,1)S(1)}, u32[]{:S(2)}, u32[]{:S(2)}) collective-permute-start(bf16[4,64,256]{2,1,0:T(8,128)(2,1)S(1)} %collective-permute-done.3.refs_1_), channel_id=1, source_target_pairs={{0,1},{1,0},{2,3},{3,2},{4,5},{5,4},{6,7},{7,6},{8,9},{9,8},{10,11... | collective-permute-start | bytes 393224 | tf_op jit(solution)/shard_map/ppermute | solution.py:23
  18.2 0.5 %shard_map.93 = (bf16[64,512]{1,0:T(8,128)(2,1)S(1)}, bf16[64,512]{1,0:T(8,128)(2,1)S(1)}) custom-call(bf16[64,1024]{1,0:T(8,128)(2,1)S(1)} %collective-permute-done.6.rows_ref.far_ref, bf16[1024,1024]{1,0:T(8,128)(2,1)S(1)} %copy-done.1), custom_call_target="tpu_custom_call" | custom-call | flops 134217728 | bytes 262144 | tf_op jit(solution)/shard_map/pallas_call | solution.py:249
  18.7 4.4 %collective-permute-done.5.refs_2_ = bf16[4,64,256]{2,1,0:T(8,128)(2,1)S(1)} collective-permute-done((bf16[4,64,256]{2,1,0:T(8,128)(2,1)S(1)}, bf16[4,64,256]{2,1,0:T(8,128)(2,1)S(1)}, u32[]{:S(2)}, u32[]{:S(2)}) %collective-permute-start.5) | collective-permute-done | bytes 131104 | tf_op jit(solution)/shard_map/ppermute | solution.py:23
  23.1 0.5 %collective-permute-start.9 = (bf16[4,64,256]{2,1,0:T(8,128)(2,1)S(1)}, bf16[4,64,256]{2,1,0:T(8,128)(2,1)S(1)}, u32[]{:S(2)}, u32[]{:S(2)}) collective-permute-start(bf16[4,64,256]{2,1,0:T(8,128)(2,1)S(1)} %collective-permute-done.5.refs_2_), channel_id=1, source_target_pairs={{0,1},{1,0},{2,3},{3,2},{4,5},{5,4},{6,7},{7,6},{8,9},{9,8},{10,11... | collective-permute-start | bytes 393224 | tf_op jit(solution)/shard_map/ppermute | solution.py:23
  23.7 0.8 %collective-permute-done.10.refs_7_ = bf16[4,64,256]{2,1,0:T(8,128)(2,1)S(1)} collective-permute-done((bf16[4,64,256]{2,1,0:T(8,128)(2,1)S(1)}, bf16[4,64,256]{2,1,0:T(8,128)(2,1)S(1)}, u32[]{:S(2)}, u32[]{:S(2)}) %collective-permute-start.10) | collective-permute-done | bytes 131104 | tf_op jit(solution)/shard_map/ppermute | solution.py:23
  24.5 0.2 collective-permute-done.9.refs_6_
  24.7 0.9 %shard_map.94 = (f32[128,512]{1,0:T(8,128)S(1)}, bf16[128,512]{1,0:T(8,128)(2,1)S(1)}) custom-call(bf16[64,512]{1,0:T(8,128)(2,1)S(1)} %get-tuple-element.29.q_own_ref, bf16[64,512]{1,0:T(8,128)(2,1)S(1)} %get-tuple-element.34.q_far_ref, bf16[4,64,256]{2,1,0:T(8,128)(2,1)S(1)} %get-tuple-element.35.refs_0_, ...), custom_call_target="tpu_custom_call" | custom-call | flops 134217728 | bytes 1048576 | tf_op jit(solution)/shard_map/pallas_call | solution.py:259
  25.6 1.3 %collective-permute-start.11 = (bf16[128,512]{1,0:T(8,128)(2,1)S(1)}, bf16[128,512]{1,0:T(8,128)(2,1)S(1)}, u32[]{:S(2)}, u32[]{:S(2)}) collective-permute-start(bf16[128,512]{1,0:T(8,128)(2,1)S(1)} %get-tuple-element.40), channel_id=1, source_target_pairs={{0,2},{1,3},{2,0},{3,1},{4,6},{5,7},{6,4},{7,5},{8,10},{9,11},{10,... | collective-permute-start | bytes 393224 | tf_op jit(solution)/shard_map/ppermute | solution.py:23
  26.9 4.5 %collective-permute-done.11.sent_ref = bf16[128,512]{1,0:T(8,128)(2,1)S(1)} collective-permute-done((bf16[128,512]{1,0:T(8,128)(2,1)S(1)}, bf16[128,512]{1,0:T(8,128)(2,1)S(1)}, u32[]{:S(2)}, u32[]{:S(2)}) %collective-permute-start.11) | collective-permute-done | bytes 131104 | tf_op jit(solution)/shard_map/ppermute | solution.py:23
  31.4 0.6 %shard_map.95.own_ref = bf16[128,1024]{1,0:T(8,128)(2,1)S(1)} custom-call(f32[128,512]{1,0:T(8,128)S(1)} %get-tuple-element.39.sum_ref, bf16[128,512]{1,0:T(8,128)(2,1)S(1)} %collective-permute-done.11.sent_ref, bf16[64,512]{1,0:T(8,128)(2,1)S(1)} %get-tuple-element.41.gate_own_ref, bf16[64,512]{1,0:T(8,128)(2,1)S(1)} %get-tuple-element.42.gate_far_ref, ...), custom_call_target="tpu_custom_call" | custom-call | flops 134217728 | bytes 1048576 | tf_op jit(solution)/shard_map/pallas_call | solution.py:267
  32.0 1.5 %collective-permute-done.12.far_ref = bf16[128,1024]{1,0:T(8,128)(2,1)S(1)} collective-permute-done((bf16[128,1024]{1,0:T(8,128)(2,1)S(1)}, bf16[128,1024]{1,0:T(8,128)(2,1)S(1)}, u32[]{:S(2)}, u32[]{:S(2)}) %collective-permute-start.12) | collective-permute-done | bytes 262176 | tf_op jit(solution)/shard_map/ppermute | solution.py:23
  33.5 1.4 %select.1 = bf16[512,1024]{1,0:T(8,128)(2,1)} custom-call(bf16[512,256]{1,0:T(8,128)(2,1)S(1)} %get-tuple-element.24.hot_ref, bf16[128,1024]{1,0:T(8,128)(2,1)S(1)} %shard_map.95.own_ref, bf16[128,1024]{1,0:T(8,128)(2,1)S(1)} %collective-permute-done.12.far_ref), custom_call_target="tpu_custom_call" | custom-call | flops 268435456 | bytes 1048576 | tf_op jit(solution)/shard_map/select/pallas_call | solution.py:275
  (20 shorter events, 0.1 us)
Async XLA Ops:
  0.0 9.2 %collective-permute-start.1 = (bf16[16,1024]{1,0:T(8,128)(2,1)}, bf16[16,1024]{1,0:T(8,128)(2,1)S(1)}, u32[]{:S(2)}, u32[]{:S(2)}) collective-permute-start(bf16[16,1024]{1,0:T(8,128)(2,1)} %param.9), channel_id=1, source_target_pairs={{0,8},{1,9},{2,10},{3,11},{4,12},{5,13},{6,14},{7,15},{8,0},{9,1},... | collective-permute-start | bytes 98312 | tf_op jit(solution)/shard_map/ppermute | solution.py:23
  4.1 5.1 %collective-permute-start = (bf16[16,1024]{1,0:T(8,128)(2,1)}, bf16[16,1024]{1,0:T(8,128)(2,1)S(1)}, u32[]{:S(2)}, u32[]{:S(2)}) collective-permute-start(bf16[16,1024]{1,0:T(8,128)(2,1)} %param.9), channel_id=1, source_target_pairs={{0,4},{1,5},{2,6},{3,7},{4,0},{5,1},{6,2},{7,3},{8,12},{9,13},{10,... | collective-permute-start | bytes 98312 | tf_op jit(solution)/shard_map/ppermute | solution.py:23
  5.6 6.2 %collective-permute-start.2 = (bf16[16,1024]{1,0:T(8,128)(2,1)}, bf16[16,1024]{1,0:T(8,128)(2,1)S(1)}, u32[]{:S(2)}, u32[]{:S(2)}) collective-permute-start(bf16[16,1024]{1,0:T(8,128)(2,1)} %param.9), channel_id=1, source_target_pairs={{0,12},{1,13},{2,14},{3,15},{4,8},{5,9},{6,10},{7,11},{8,4},{9,5},... | collective-permute-start | bytes 98312 | tf_op jit(solution)/shard_map/ppermute | solution.py:23
  7.5 10.2 %collective-permute-start.3 = (bf16[4,64,256]{2,1,0:T(8,128)(2,1)S(1)}, bf16[4,64,256]{2,1,0:T(8,128)(2,1)S(1)}, u32[]{:S(2)}, u32[]{:S(2)}) collective-permute-start(bf16[4,64,256]{2,1,0:T(8,128)(2,1)S(1)} %get-tuple-element.25), channel_id=1, source_target_pairs={{0,4},{1,5},{2,6},{3,7},{4,0},{5,1},{6,2},{7,3},{8,12},{9,13},{10,... | collective-permute-start | bytes 393224 | tf_op jit(solution)/shard_map/ppermute | solution.py:23
  11.9 6.4 %collective-permute-start.6 = (bf16[64,1024]{1,0:T(8,128)(2,1)S(1)}, bf16[64,1024]{1,0:T(8,128)(2,1)S(1)}, u32[]{:S(2)}, u32[]{:S(2)}) collective-permute-start(bf16[64,1024]{1,0:T(8,128)(2,1)S(1)} %constant_dynamic-update-slice_fusion.rows_ref.own_ref), channel_id=1, source_target_pairs={{0,2},{1,3},{2,0},{3,1},{4,6},{5,7},{6,4},{7,5},{8,10},{9,11},{10,... | collective-permute-start | bytes 393224 | tf_op jit(solution)/shard_map/ppermute | solution.py:23
  13.4 9.7 %collective-permute-start.5 = (bf16[4,64,256]{2,1,0:T(8,128)(2,1)S(1)}, bf16[4,64,256]{2,1,0:T(8,128)(2,1)S(1)}, u32[]{:S(2)}, u32[]{:S(2)}) collective-permute-start(bf16[4,64,256]{2,1,0:T(8,128)(2,1)S(1)} %get-tuple-element.31), channel_id=1, source_target_pairs={{0,8},{1,9},{2,10},{3,11},{4,12},{5,13},{6,14},{7,15},{8,0},{9,1},... | collective-permute-start | bytes 393224 | tf_op jit(solution)/shard_map/ppermute | solution.py:23
  14.3 8.8 %collective-permute-start.4 = (bf16[4,64,256]{2,1,0:T(8,128)(2,1)S(1)}, bf16[4,64,256]{2,1,0:T(8,128)(2,1)S(1)}, u32[]{:S(2)}, u32[]{:S(2)}) collective-permute-start(bf16[4,64,256]{2,1,0:T(8,128)(2,1)S(1)} %get-tuple-element.30), channel_id=1, source_target_pairs={{0,12},{1,13},{2,14},{3,15},{4,8},{5,9},{6,10},{7,11},{8,4},{9,5},... | collective-permute-start | bytes 393224 | tf_op jit(solution)/shard_map/ppermute | solution.py:23
  14.6 1.6 %copy-start = (bf16[1024,1024]{1,0:T(8,128)(2,1)S(1)}, bf16[1024,1024]{1,0:T(8,128)(2,1)}, u32[]{:S(2)}) copy-start(bf16[1024,1024]{1,0:T(8,128)(2,1)} %w_ref.4) | copy-start | bytes 6291460
  16.2 2.0 %copy-start.1 = (bf16[1024,1024]{1,0:T(8,128)(2,1)S(1)}, bf16[1024,1024]{1,0:T(8,128)(2,1)}, u32[]{:S(2)}) copy-start(bf16[1024,1024]{1,0:T(8,128)(2,1)} %w_ref.4) | copy-start | bytes 6291460
  17.6 13.8 %copy-start.2 = (bf16[512,1024]{1,0:T(8,128)(2,1)S(1)}, bf16[512,1024]{1,0:T(8,128)(2,1)}, u32[]{:S(2)}) copy-start(bf16[512,1024]{1,0:T(8,128)(2,1)} %w_ref.5) | copy-start | bytes 3145732
  17.6 13.8 %copy-start.3 = (f32[512]{0:T(512)S(1)}, f32[512]{0:T(512)}, u32[]{:S(2)}) copy-start(f32[512]{0:T(512)} %param.13) | copy-start | bytes 6148
  17.6 6.0 %collective-permute-start.7 = (bf16[4,64,256]{2,1,0:T(8,128)(2,1)S(1)}, bf16[4,64,256]{2,1,0:T(8,128)(2,1)S(1)}, u32[]{:S(2)}, u32[]{:S(2)}) collective-permute-start(bf16[4,64,256]{2,1,0:T(8,128)(2,1)S(1)} %get-tuple-element.35.refs_0_), channel_id=1, source_target_pairs={{0,1},{1,0},{2,3},{3,2},{4,5},{5,4},{6,7},{7,6},{8,9},{9,8},{10,11... | collective-permute-start | bytes 393224 | tf_op jit(solution)/shard_map/ppermute | solution.py:23
  17.7 6.0 %collective-permute-start.8 = (bf16[4,64,256]{2,1,0:T(8,128)(2,1)S(1)}, bf16[4,64,256]{2,1,0:T(8,128)(2,1)S(1)}, u32[]{:S(2)}, u32[]{:S(2)}) collective-permute-start(bf16[4,64,256]{2,1,0:T(8,128)(2,1)S(1)} %collective-permute-done.3.refs_1_), channel_id=1, source_target_pairs={{0,1},{1,0},{2,3},{3,2},{4,5},{5,4},{6,7},{7,6},{8,9},{9,8},{10,11... | collective-permute-start | bytes 393224 | tf_op jit(solution)/shard_map/ppermute | solution.py:23
  23.1 1.3 %collective-permute-start.10 = (bf16[4,64,256]{2,1,0:T(8,128)(2,1)S(1)}, bf16[4,64,256]{2,1,0:T(8,128)(2,1)S(1)}, u32[]{:S(2)}, u32[]{:S(2)}) collective-permute-start(bf16[4,64,256]{2,1,0:T(8,128)(2,1)S(1)} %collective-permute-done.4.refs_3_), channel_id=1, source_target_pairs={{0,1},{1,0},{2,3},{3,2},{4,5},{5,4},{6,7},{7,6},{8,9},{9,8},{10,11... | collective-permute-start | bytes 393224 | tf_op jit(solution)/shard_map/ppermute | solution.py:23
  23.1 1.5 %collective-permute-start.9 = (bf16[4,64,256]{2,1,0:T(8,128)(2,1)S(1)}, bf16[4,64,256]{2,1,0:T(8,128)(2,1)S(1)}, u32[]{:S(2)}, u32[]{:S(2)}) collective-permute-start(bf16[4,64,256]{2,1,0:T(8,128)(2,1)S(1)} %collective-permute-done.5.refs_2_), channel_id=1, source_target_pairs={{0,1},{1,0},{2,3},{3,2},{4,5},{5,4},{6,7},{7,6},{8,9},{9,8},{10,11... | collective-permute-start | bytes 393224 | tf_op jit(solution)/shard_map/ppermute | solution.py:23
  25.6 5.8 %collective-permute-start.11 = (bf16[128,512]{1,0:T(8,128)(2,1)S(1)}, bf16[128,512]{1,0:T(8,128)(2,1)S(1)}, u32[]{:S(2)}, u32[]{:S(2)}) collective-permute-start(bf16[128,512]{1,0:T(8,128)(2,1)S(1)} %get-tuple-element.40), channel_id=1, source_target_pairs={{0,2},{1,3},{2,0},{3,1},{4,6},{5,7},{6,4},{7,5},{8,10},{9,11},{10,... | collective-permute-start | bytes 393224 | tf_op jit(solution)/shard_map/ppermute | solution.py:23
  31.9 1.6 %collective-permute-start.12 = (bf16[128,1024]{1,0:T(8,128)(2,1)S(1)}, bf16[128,1024]{1,0:T(8,128)(2,1)S(1)}, u32[]{:S(2)}, u32[]{:S(2)}) collective-permute-start(bf16[128,1024]{1,0:T(8,128)(2,1)S(1)} %shard_map.95.own_ref), channel_id=1, source_target_pairs={{0,1},{1,0},{2,3},{3,2},{4,5},{5,4},{6,7},{7,6},{8,9},{9,8},{10,11... | collective-permute-start | bytes 786440 | tf_op jit(solution)/shard_map/ppermute | solution.py:23
where the time goes:
time: 35.2 us; the launch traced here: 35 us
  waiting for transfers between devices  14.1 us (40%)
  starting transfers between devices  11.7 us (33%)
  Pallas kernels  6.62 us (19%)
  local copies, waits for them, and re-layouts  2.38 us (7%)
    ppermute x13, waiting for transfers between devices, swap_with(): lax.ppermute(shard, 'rank', [(i, i ^ mask) for i in range(lax.axis_size('...  14.1 us
    ppermute x13, starting transfers between devices, swap_with(): lax.ppermute(shard, 'rank', [(i, i ^ mask) for i in range(lax.axis_size('...  11.7 us
    unnamed x11, local copies, waits for them, and re-layouts  2.37 us
    pallas_call x1, Pallas kernels, layer(): call(functools.partial(pick_kernel, groups, size), [shape((heads, block,...  1.84 us
    pallas_call x1, Pallas kernels, layer(): pl.pallas_call(select_kernel, out_shape=shape((share, width), jnp.bfloat1...  1.43 us
    pallas_call x1, Pallas kernels, layer(): call(functools.partial(project_and_place_kernel, heads, size, pool_here),...  1.41 us
    pallas_call x1, Pallas kernels, layer(): call(functools.partial(attend_kernel, 1.0 / math.sqrt(dim)), [shape((rows...  0.88 us
  transfers between devices with their start and end apart: 13, of which 6 were waited for; matrix products, arithmetic and copies ran while one was open for 2% of the time, Pallas kernels for 11%

commit v1 on v0

v1 whole, which is shorter than its diff:
```python
import functools
import math

import jax
import jax.numpy as jnp
from jax import lax
from jax.experimental import pallas as pl
from jax.experimental.pallas import tpu as pltpu
from jax.sharding import PartitionSpec as P


norm_eps = 1e-05
VMEM = pl.BlockSpec(memory_space=pltpu.VMEM)
SMEM = pl.BlockSpec(memory_space=pltpu.SMEM)
HBM = pl.BlockSpec(memory_space=pltpu.HBM)


def in_hbm(array):
    return pltpu.with_memory_space_constraint(array, pltpu.HBM)


def swap_with(shard, mask):
    return lax.ppermute(shard, "rank", [(i, i ^ mask) for i in range(lax.axis_size("rank"))])


def call(kernel, out_shape, in_specs, scratch=(), flops=0, bytes_accessed=0):
    single = not isinstance(out_shape, (list, tuple))
    return pl.pallas_call(
        kernel,
        out_shape=out_shape,
        in_specs=in_specs,
        out_specs=VMEM if single else [VMEM] * len(out_shape),
        scratch_shapes=list(scratch),
        compiler_params=pltpu.CompilerParams(vmem_limit_bytes=24 * 1024 * 1024),
        cost_estimate=pl.CostEstimate(flops=flops, bytes_accessed=bytes_accessed, transcendentals=0),
    )


def pick_kernel(groups, size, me_ref, ranker_ref, length_ref, slot_ref, pool_ref, kv_ref, *refs):
    keep_ref, give_ref, rows_ref, ranker, length, slots, held, sem = refs
    slots_here, heads, _, _ = kv_ref.shape
    count = heads // 2
    core = me_ref[0] % 2
    users, blocks = slots.shape
    pairs = ((ranker_ref, ranker), (length_ref, length), (slot_ref, slots), (pool_ref, rows_ref), (kv_ref, held))
    loads = [pltpu.make_async_copy(ref, to, sem.at[i]) for i, (ref, to) in enumerate(pairs)]
    for load in loads:
        load.start()
    for load in loads[:3]:
        load.wait()
    first = me_ref[0] * slots_here
    my_group = me_ref[0] // size

    def held_by(user):
        def step(b, found):
            local = slots[user, b] - first
            here = (local >= 0) & (local < slots_here)
            return jnp.where(here, local, found[0]), jnp.where(here, b, found[1])

        return lax.fori_loop(0, blocks, step, (0, 0), unroll=blocks <= 16)

    def user_of(group):
        def step(u, found):
            return jnp.where(ranker[u] == group, u, found)

        return lax.fori_loop(0, users, step, 0, unroll=users <= 16)

    chosen = []
    for k in range(groups):
        user = user_of(my_group ^ k)
        slot, at = held_by(user)
        chosen.append((slot, at < length[user]))
    for load in loads[3:]:
        load.wait()
    for k, (slot, live) in enumerate(chosen):
        for i in range(count):
            for out_ref, half in ((keep_ref, core), (give_ref, 1 - core)):
                taken = held[slot, half * count + i]
                out_ref[k, i] = jnp.where(live, taken, jnp.zeros_like(taken))


def pack_kernel(keep_ref, got_ref, *outs):
    for k, out in enumerate(outs):
        out[0] = keep_ref[k]
        out[1] = got_ref[k]


def project(core, heads, rows_ref, w_ref, q_ref, gate_ref, give_ref, halves):
    dim = w_ref.shape[1] // (2 * heads)
    part = heads // 2 * dim
    qu = jax.nn.silu(jnp.dot(rows_ref[...], w_ref[...], preferred_element_type=jnp.float32))
    qu = qu.astype(jnp.bfloat16)
    for h in range(heads):
        at = (2 * h) // heads
        cols = slice(h * dim - at * part, (h + 1) * dim - at * part)
        halves[at, :, cols] = qu[:, 2 * h * dim : (2 * h + 1) * dim]
        gate = qu[:, (2 * h + 1) * dim : (2 * h + 2) * dim]
        gate_ref[:, h * dim : (h + 1) * dim] = gate
        give_ref[:, part + h * dim : part + (h + 1) * dim] = gate
    q_ref[...] = halves[core]
    give_ref[:, :part] = halves[1 - core]
    give_ref[:, 3 * part :] = rows_ref[...]


def project_kernel(heads, me_ref, rows_ref, w_ref, q_ref, gate_ref, give_ref, halves):
    project(me_ref[0] % 2, heads, rows_ref, w_ref, q_ref, gate_ref, give_ref, halves)


def project_and_place_kernel(
    heads, size, me_ref, rows_ref, w_ref, ranker_ref, ids_ref, q_ref, gate_ref, give_ref, hot_ref, halves, ranker, ids, sem
):
    users = ids_ref.shape[0]
    share = ids.shape[1]
    me = me_ref[0]
    my_group, my_place = me // size, me % size
    loads = (
        pltpu.make_async_copy(ranker_ref, ranker, sem.at[0]),
        pltpu.make_async_copy(ids_ref.at[:, pl.ds(pl.multiple_of(my_place * share, share), share)], ids, sem.at[1]),
    )
    for load in loads:
        load.start()
    project(me % 2, heads, rows_ref, w_ref, q_ref, gate_ref, give_ref, halves)
    for load in loads:
        load.wait()

    def step(u, found):
        return jnp.where(ranker[u] == my_group, u, found)

    my_user = lax.fori_loop(0, users, step, 0, unroll=users <= 16)
    item = ids[pl.ds(my_user, 1), :]
    half = rows_ref.shape[0]
    groups = ranker.shape[0]
    pool_here = half // groups
    owner = item // pool_here
    differs = (owner % size) ^ my_place
    place = (differs % 2) * 2 * half + (differs // 2) * half
    apart = (owner // size) ^ my_group
    bit = 1
    while bit < groups:
        place = place + (apart // bit % 2) * (groups // (2 * bit)) * pool_here
        bit *= 2
    place = place + item % pool_here
    part = math.gcd(4 * half, 256)
    for first in range(0, 4 * half, part):
        at = lax.broadcasted_iota(jnp.int32, (part, share), 0) + first
        hot = jnp.where(at == place, 1.0, 0.0)
        hot_ref[:, first : first + part] = jnp.transpose(hot).astype(jnp.bfloat16)


def attend_kernel(scale, q_own_ref, q_far_ref, other_own_ref, other_far_ref, *refs):
    kv, sum_ref, sent_ref = refs[:-2], refs[-2], refs[-1]
    sources, count, _, pair = kv[0].shape
    dim = pair // 2
    half = q_own_ref.shape[0]
    tile = math.gcd(half, 64)
    spots = [(ref, i) for ref in kv for i in range(sources)]
    together = math.gcd(len(spots), 8)

    def one_tile(t, _):
        at = pl.ds(pl.multiple_of(t * tile, tile), tile)
        for h in range(count):
            cols = slice(h * dim, (h + 1) * dim)
            query = jnp.concatenate(
                [ref[at, cols] for ref in (q_own_ref, q_far_ref, other_own_ref, other_far_ref)], axis=0
            )
            total = None
            for first in range(0, len(spots), together):
                parts = [ref[i, h] for ref, i in spots[first : first + together]]
                keys = jnp.concatenate([p[:, :dim] for p in parts], axis=0)
                values = jnp.concatenate([p[:, dim:] for p in parts], axis=0)
                scores = lax.dot_general(
                    query, keys, (((1,), (1,)), ((), ())), preferred_element_type=jnp.float32
                )
                weights = jax.nn.silu(scores * scale).astype(jnp.bfloat16)
                add = jnp.dot(weights, values, preferred_element_type=jnp.float32)
                total = add if total is None else total + add
            for i in range(4):
                here = pl.ds(pl.multiple_of(t * tile + i * half, tile), tile)
                piece = total[i * tile : (i + 1) * tile]
                sum_ref[here, cols] = piece
                sent_ref[here, cols] = piece.astype(jnp.bfloat16)
        return 0

    lax.fori_loop(0, half // tile, one_tile, 0, unroll=half == tile)


def combine_kernel(sum_ref, got_ref, out_ref):
    half = sum_ref.shape[0] // 4
    for i in range(4):
        here, there = slice(i * half, (i + 1) * half), slice((i ^ 1) * half, ((i ^ 1) + 1) * half)
        out_ref[here, :] = sum_ref[here, :] + got_ref[there, :].astype(jnp.float32)


def finish_kernel(
    me_ref, att_ref, far_ref, gate_own_ref, gate_far_ref, own_ref, far_rows_ref, other_own_ref, other_far_ref,
    gain_ref, w_ref, hot_ref, out_ref, table, buffer, sem
):
    core = me_ref[0] % 2
    half, width = own_ref.shape
    part = att_ref.shape[1]
    tile = math.gcd(half, 64)
    w_mine = w_ref[pl.ds(pl.multiple_of(core * part, part), part), :]
    w_other = w_ref[pl.ds(pl.multiple_of((1 - core) * part, part), part), :]
    low, high = gain_ref[:, :part], gain_ref[:, part:]
    gain_mine, gain_other = jnp.where(core == 0, low, high), jnp.where(core == 0, high, low)
    pieces = (
        (gate_own_ref, 0, own_ref, 0),
        (gate_far_ref, 0, far_rows_ref, 0),
        (other_own_ref, part, other_own_ref, 3 * part),
        (other_far_ref, part, other_far_ref, 3 * part),
    )
    for i, (gates, gate_at, rows, rows_at) in enumerate(pieces):
        for first in range(0, half, tile):
            mine = slice(i * half + first, i * half + first + tile)
            theirs = slice((i ^ 2) * half + first, (i ^ 2) * half + first + tile)
            here = slice(first, first + tile)
            a, b = att_ref[mine, :], far_ref[theirs, :]
            mean = (jnp.sum(a, axis=1, keepdims=True) + jnp.sum(b, axis=1, keepdims=True)) * (0.5 / part)
            square = (jnp.sum(a * a, axis=1, keepdims=True) + jnp.sum(b * b, axis=1, keepdims=True)) * (0.5 / part)
            factor = lax.rsqrt(square - mean * mean + norm_eps)
            low = gates[here, gate_at : gate_at + part].astype(jnp.float32)
            high = gates[here, gate_at + part : gate_at + 2 * part].astype(jnp.float32)
            g_mine, g_other = jnp.where(core == 0, low, high), jnp.where(core == 0, high, low)
            a = ((a - mean) * factor * gain_mine * g_mine).astype(jnp.bfloat16)
            b = ((b - mean) * factor * gain_other * g_other).astype(jnp.bfloat16)
            mixed = jnp.dot(a, w_mine, preferred_element_type=jnp.float32)
            mixed = mixed + jnp.dot(b, w_other, preferred_element_type=jnp.float32)
            mixed = mixed + rows[here, rows_at : rows_at + width].astype(jnp.float32)
            table[mine, :] = mixed.astype(jnp.bfloat16)
    share = hot_ref.shape[0]
    tile = math.gcd(share, 128)
    copies = []
    for i, first in enumerate(range(0, share, tile)):
        at = slice(first, first + tile)
        buffer[at, :] = jnp.dot(hot_ref[at, :], table[...], preferred_element_type=jnp.float32).astype(jnp.bfloat16)
        copies.append(pltpu.make_async_copy(buffer.at[at], out_ref.at[at], sem.at[i]))
        copies[-1].start()
    for copy in copies:
        copy.wait()


def layer(pool, kv_cache, w_qu, w_out, norm_gain, cand_ids, ranker, hist_blocks, cache_slot):
    devices = lax.axis_size("rank")
    me = lax.axis_index("rank").astype(jnp.int32).reshape(1)
    _, heads, block, pair = kv_cache.shape
    dim = pair // 2
    users, _ = cache_slot.shape
    _, width = pool.shape
    groups = users
    size = devices // groups
    assert size == 4 and groups & (groups - 1) == 0
    shape = jax.ShapeDtypeStruct
    dma = pltpu.SemaphoreType.DMA

    count = heads // 2
    blocks_shape = shape((groups, count, block, pair), jnp.bfloat16)
    keep, give, pool_rows = call(
        functools.partial(pick_kernel, groups, size),
        [blocks_shape, blocks_shape, shape(pool.shape, pool.dtype)],
        [SMEM] + [HBM] * 5,
        [
            pltpu.SMEM(ranker.shape, jnp.int32),
            pltpu.SMEM(hist_blocks.shape, jnp.int32),
            pltpu.SMEM(cache_slot.shape, jnp.int32),
            pltpu.VMEM(kv_cache.shape, kv_cache.dtype),
            dma((5,)),
        ],
        bytes_accessed=2 * kv_cache.size * 2,
    )(me, *[in_hbm(a) for a in (ranker, hist_blocks, cache_slot, pool, kv_cache)])
    got = swap_with(give, 1)
    own_rows, sent = pool_rows, pool
    bit = groups // 2
    while bit:
        if bit < groups // 2:
            sent, got = lax.optimization_barrier((own_rows, got))
        own_rows = jnp.concatenate([own_rows, swap_with(sent, size * bit)], axis=0)
        bit //= 2
    kv = call(pack_kernel, [shape((2, count, block, pair), jnp.bfloat16)] * groups, [VMEM] * 2)(keep, got)
    kv = list(kv)
    for k in range(1, groups):
        kv[k] = swap_with(kv[k], size * k)

    far_rows = swap_with(own_rows, 2)
    half = own_rows.shape[0]
    rows = 4 * half
    part = count * dim
    share = cand_ids.shape[1] // size
    cost = dict(flops=2 * half * width * w_qu.shape[1], bytes_accessed=half * width * 4)
    outs = [shape((half, n), jnp.bfloat16) for n in (part, 2 * part, 3 * part + width)]
    halves = pltpu.VMEM((2, half, part), jnp.bfloat16)
    q_own, gate_own, give_own, hot = call(
        functools.partial(project_and_place_kernel, heads, size),
        outs + [shape((share, rows), jnp.bfloat16)],
        [SMEM, VMEM, VMEM, HBM, HBM],
        [halves, pltpu.SMEM(ranker.shape, jnp.int32), pltpu.VMEM((users, share), jnp.int32), dma((2,))],
        **cost,
    )(me, own_rows, w_qu, in_hbm(ranker), in_hbm(cand_ids))
    other_own = swap_with(give_own, 1)
    q_far, gate_far, give_far = call(
        functools.partial(project_kernel, heads), outs, [SMEM, VMEM, VMEM], [halves], **cost
    )(me, far_rows, w_qu)
    other_far = swap_with(give_far, 1)

    sums, sent = call(
        functools.partial(attend_kernel, 1.0 / math.sqrt(dim)),
        [shape((rows, part), jnp.float32), shape((rows, part), jnp.bfloat16)],
        [VMEM] * (4 + groups),
        flops=4 * rows * 2 * groups * block * part,
        bytes_accessed=2 * groups * count * block * pair * 2,
    )(q_own, q_far, other_own, other_far, *kv)
    sent = swap_with(sent, 2)
    attended = call(combine_kernel, shape((rows, part), jnp.float32), [VMEM] * 2)(sums, sent)
    other = swap_with(attended, 1)
    return pl.pallas_call(
        finish_kernel,
        out_shape=shape((share, width), jnp.bfloat16),
        in_specs=[SMEM] + [VMEM] * 11,
        out_specs=HBM,
        scratch_shapes=[
            pltpu.VMEM((rows, width), jnp.bfloat16),
            pltpu.VMEM((share, width), jnp.bfloat16),
            dma((share // math.gcd(share, 128),)),
        ],
        compiler_params=pltpu.CompilerParams(vmem_limit_bytes=24 * 1024 * 1024),
        cost_estimate=pl.CostEstimate(
            flops=2 * (share * rows + rows * heads * dim) * width, bytes_accessed=share * width * 2, transcendentals=0
        ),
        name="finish",
    )(
        me, attended, other, gate_own, gate_far, own_rows, far_rows, other_own, other_far,
        norm_gain[None, :], w_out, hot,
    )


def solution(mesh):
    in_specs = (
        P(("groups", "rank"), None),
        P(("groups", "rank"), None, None, None),
        P(),
        P(),
        P(),
        P("groups", None),
        P(),
        P("groups"),
        P("groups", None),
    )
    out_specs = P(("groups", "rank"), None)
    return jax.shard_map(layer, mesh=mesh, in_specs=in_specs, out_specs=out_specs, check_vma=False)
```

time: 35.2 us -> 42.3 us (1.20)
  waiting for transfers between devices: 14.1 us -> 20.1 us
  starting transfers between devices: 11.7 us -> 14.5 us
  Pallas kernels: 6.62 us -> 5.52 us
  local copies, waits for them, and re-layouts: 2.38 us -> 1.62 us
    ppermute x13 -> x11, waiting for transfers between devices: 14.1 us -> 20.1 us  [swap_with(): lax.ppermute(shard, 'rank', [(i, i ^ mask) for i in range(lax.axis_size('...]
    ppermute x13 -> x11, starting transfers between devices: 11.7 us -> 14.5 us  [swap_with(): lax.ppermute(shard, 'rank', [(i, i ^ mask) for i in range(lax.axis_size('...]
    pallas_call x5 -> x6, Pallas kernels: 5.74 us -> 4.91 us  [the longest x1 2.12 us: layer(): pl.pallas_call(finish_kernel, out_shape=shape((share, width), jnp.bfloat1...]
    unnamed x11 -> x10, local copies, waits for them, and re-layouts: 2.37 us -> 1.61 us
  transfers between devices with their start and end apart: 13 -> 11, of which waited for: 6 -> 7; matrix products, arithmetic and copies ran while one was open for 2% -> 0% of each run, Pallas kernels for 11% -> 4%
where the time goes in v1:
time: 42.3 us; the launch traced here: 41.8 us
  waiting for transfers between devices  20.1 us (48%)
  starting transfers between devices  14.5 us (34%)
  Pallas kernels  5.52 us (13%)
  local copies, waits for them, and re-layouts  1.62 us (4%)
    ppermute x11, waiting for transfers between devices, swap_with(): lax.ppermute(shard, 'rank', [(i, i ^ mask) for i in range(lax.axis_size('...  20.1 us
    ppermute x11, starting transfers between devices, swap_with(): lax.ppermute(shard, 'rank', [(i, i ^ mask) for i in range(lax.axis_size('...  14.5 us
    pallas_call x1, Pallas kernels, layer(): pl.pallas_call(finish_kernel, out_shape=shape((share, width), jnp.bfloat1...  2.12 us
    unnamed x10, local copies, waits for them, and re-layouts  1.61 us
    pallas_call x1, Pallas kernels, layer(): call(functools.partial(pick_kernel, groups, size), [blocks_shape, blocks_...  1.17 us
    pallas_call x1, Pallas kernels, layer(): call(functools.partial(project_and_place_kernel, heads, size), outs + [sh...  1.04 us
  transfers between devices with their start and end apart: 11, of which 7 were waited for; matrix products, arithmetic and copies ran while one was open for 0% of the time, Pallas kernels for 4%

profile of v1, /device:TPU:0, one launch (start us, length us, event | category | flops | bytes accessed | tf_op | source)
XLA Modules:
  0.0 41.8 jit_solution(13459962812591019164)
XLA Ops:
  0.0 1.2 %shard_map.91 = (bf16[4,2,64,256]{3,2,1,0:T(8,128)(2,1)S(1)}, bf16[4,2,64,256]{3,2,1,0:T(8,128)(2,1)S(1)}, bf16[16,1024]{1,0:T(8,128)(2,1)S(1)}) custom-call(s32[1]{0:T(128)} %bitcast.me_ref, s32[4]{0:T(128)} %ranker_ref.3, s32[4]{0:T(128)} %length_ref.1, s32[4,16]{1,0:T(4,128)} %slot_ref.1, bf16[16,1024]{1,0:T(8,128)(2,1)} %pool_ref.1, ...), custom_call_target="tpu_custom_call" | custom-call | bytes 1048576 | tf_op jit(solution)/shard_map/pallas_call | solution.py:257
  1.2 0.6 %collective-permute-start.1 = (bf16[4,2,64,256]{3,2,1,0:T(8,128)(2,1)S(1)}, bf16[4,2,64,256]{3,2,1,0:T(8,128)(2,1)S(1)}, u32[]{:S(2)}, u32[]{:S(2)}) collective-permute-start(bf16[4,2,64,256]{3,2,1,0:T(8,128)(2,1)S(1)} %get-tuple-element.24), channel_id=1, source_target_pairs={{0,1},{1,0},{2,3},{3,2},{4,5},{5,4},{6,7},{7,6},{8,9},{9,8},{10,11... | collective-permute-start | bytes 786440 | tf_op jit(solution)/shard_map/ppermute | solution.py:23
  1.7 3.7 %collective-permute-start = (bf16[16,1024]{1,0:T(8,128)(2,1)}, bf16[16,1024]{1,0:T(8,128)(2,1)S(1)}, u32[]{:S(2)}, u32[]{:S(2)}) collective-permute-start(bf16[16,1024]{1,0:T(8,128)(2,1)} %pool_ref.1), channel_id=1, source_target_pairs={{0,8},{1,9},{2,10},{3,11},{4,12},{5,13},{6,14},{7,15},{8,0},{9,1},... | collective-permute-start | bytes 98312 | tf_op jit(solution)/shard_map/ppermute | solution.py:23
  5.4 2.2 %collective-permute-done = bf16[16,1024]{1,0:T(8,128)(2,1)S(1)} collective-permute-done((bf16[16,1024]{1,0:T(8,128)(2,1)}, bf16[16,1024]{1,0:T(8,128)(2,1)S(1)}, u32[]{:S(2)}, u32[]{:S(2)}) %collective-permute-start) | collective-permute-done | bytes 32800 | tf_op jit(solution)/shard_map/ppermute | solution.py:23
  7.6 1.9 %collective-permute-start.2 = (bf16[32,1024]{1,0:T(8,128)(2,1)S(1)}, bf16[32,1024]{1,0:T(8,128)(2,1)S(1)}, u32[]{:S(2)}, u32[]{:S(2)}) collective-permute-start(bf16[32,1024]{1,0:T(8,128)(2,1)S(1)} %pad_maximum_fusion), channel_id=1, source_target_pairs={{0,4},{1,5},{2,6},{3,7},{4,0},{5,1},{6,2},{7,3},{8,12},{9,13},{10,... | collective-permute-start | bytes 196616 | tf_op jit(solution)/shard_map/ppermute | solution.py:23
  9.5 2.4 %collective-permute-done.2 = bf16[32,1024]{1,0:T(8,128)(2,1)S(1)} collective-permute-done((bf16[32,1024]{1,0:T(8,128)(2,1)S(1)}, bf16[32,1024]{1,0:T(8,128)(2,1)S(1)}, u32[]{:S(2)}, u32[]{:S(2)}) %collective-permute-start.2) | collective-permute-done | bytes 65568 | tf_op jit(solution)/shard_map/ppermute | solution.py:23
  11.9 1.7 %collective-permute-start.3 = (bf16[64,1024]{1,0:T(8,128)(2,1)S(1)}, bf16[64,1024]{1,0:T(8,128)(2,1)S(1)}, u32[]{:S(2)}, u32[]{:S(2)}) collective-permute-start(bf16[64,1024]{1,0:T(8,128)(2,1)S(1)} %constant_dynamic-update-slice_fusion.rows_ref.own_ref), channel_id=1, source_target_pairs={{0,2},{1,3},{2,0},{3,1},{4,6},{5,7},{6,4},{7,5},{8,10},{9,11},{10,... | collective-permute-start | bytes 393224 | tf_op jit(solution)/shard_map/ppermute | solution.py:23
  13.7 1.6 %copy-done = bf16[1024,1024]{1,0:T(8,128)(2,1)S(1)} copy-done((bf16[1024,1024]{1,0:T(8,128)(2,1)S(1)}, bf16[1024,1024]{1,0:T(8,128)(2,1)}, u32[]{:S(2)}) %copy-start) | copy-done | bytes 2097176
  15.3 1.0 %shard_map.92 = (bf16[64,256]{1,0:T(8,128)(2,1)S(1)}, bf16[64,512]{1,0:T(8,128)(2,1)S(1)}, bf16[64,1792]{1,0:T(8,128)(2,1)S(1)}, bf16[512,256]{1,0:T(8,128)(2,1)S(1)}) custom-call(s32[1]{0:T(128)} %bitcast.me_ref, bf16[64,1024]{1,0:T(8,128)(2,1)S(1)} %constant_dynamic-update-slice_fusion.rows_ref.own_ref, bf16[1024,1024]{1,0:T(8,128)(2,1)S(1)} %copy-done, ...), custom_call_target="tpu_custom_call" | custom-call | flops 134217728 | bytes 262144 | tf_op jit(solution)/shard_map/pallas_call | solution.py:291
  16.3 0.0 copy-start.3
  16.3 0.1 collective-permute-start.4
  16.4 0.5 %collective-permute-done.3.rows_ref.far_rows_ref = bf16[64,1024]{1,0:T(8,128)(2,1)S(1)} collective-permute-done((bf16[64,1024]{1,0:T(8,128)(2,1)S(1)}, bf16[64,1024]{1,0:T(8,128)(2,1)S(1)}, u32[]{:S(2)}, u32[]{:S(2)}) %collective-permute-start.3) | collective-permute-done | bytes 131104 | tf_op jit(solution)/shard_map/ppermute | solution.py:23
  16.9 0.5 %shard_map.93 = (bf16[64,256]{1,0:T(8,128)(2,1)S(1)}, bf16[64,512]{1,0:T(8,128)(2,1)S(1)}, bf16[64,1792]{1,0:T(8,128)(2,1)S(1)}) custom-call(s32[1]{0:T(128)} %bitcast.me_ref, bf16[64,1024]{1,0:T(8,128)(2,1)S(1)} %collective-permute-done.3.rows_ref.far_rows_ref, bf16[1024,1024]{1,0:T(8,128)(2,1)S(1)} %copy-done.1), custom_call_target="tpu_custom_call" | custom-call | flops 134217728 | bytes 262144 | tf_op jit(solution)/shard_map/pallas_call | solution.py:299
  17.4 0.1 collective-permute-start.5
  17.5 1.9 %collective-permute-start.6 = (bf16[2,2,64,256]{3,2,1,0:T(8,128)(2,1)S(1)}, bf16[2,2,64,256]{3,2,1,0:T(8,128)(2,1)S(1)}, u32[]{:S(2)}, u32[]{:S(2)}) collective-permute-start(bf16[2,2,64,256]{3,2,1,0:T(8,128)(2,1)S(1)} %get-tuple-element.33), channel_id=1, source_target_pairs={{0,4},{1,5},{2,6},{3,7},{4,0},{5,1},{6,2},{7,3},{8,12},{9,13},{10,... | collective-permute-start | bytes 393224 | tf_op jit(solution)/shard_map/ppermute | solution.py:23
  19.4 3.0 %collective-permute-start.7 = (bf16[2,2,64,256]{3,2,1,0:T(8,128)(2,1)S(1)}, bf16[2,2,64,256]{3,2,1,0:T(8,128)(2,1)S(1)}, u32[]{:S(2)}, u32[]{:S(2)}) collective-permute-start(bf16[2,2,64,256]{3,2,1,0:T(8,128)(2,1)S(1)} %get-tuple-element.34), channel_id=1, source_target_pairs={{0,8},{1,9},{2,10},{3,11},{4,12},{5,13},{6,14},{7,15},{8,0},{9,1},... | collective-permute-start | bytes 393224 | tf_op jit(solution)/shard_map/ppermute | solution.py:23
  22.4 1.2 %collective-permute-done.6.refs_1_ = bf16[2,2,64,256]{3,2,1,0:T(8,128)(2,1)S(1)} collective-permute-done((bf16[2,2,64,256]{3,2,1,0:T(8,128)(2,1)S(1)}, bf16[2,2,64,256]{3,2,1,0:T(8,128)(2,1)S(1)}, u32[]{:S(2)}, u32[]{:S(2)}) %collective-permute-start.6) | collective-permute-done | bytes 131104 | tf_op jit(solution)/shard_map/ppermute | solution.py:23
  23.6 8.8 %collective-permute-done.7.refs_2_ = bf16[2,2,64,256]{3,2,1,0:T(8,128)(2,1)S(1)} collective-permute-done((bf16[2,2,64,256]{3,2,1,0:T(8,128)(2,1)S(1)}, bf16[2,2,64,256]{3,2,1,0:T(8,128)(2,1)S(1)}, u32[]{:S(2)}, u32[]{:S(2)}) %collective-permute-start.7) | collective-permute-done | bytes 131104 | tf_op jit(solution)/shard_map/ppermute | solution.py:23
  32.4 0.6 %shard_map.95 = (f32[256,256]{1,0:T(8,128)S(1)}, bf16[256,256]{1,0:T(8,128)(2,1)S(1)}) custom-call(bf16[64,256]{1,0:T(8,128)(2,1)S(1)} %get-tuple-element.26.q_own_ref, bf16[64,256]{1,0:T(8,128)(2,1)S(1)} %get-tuple-element.27.q_far_ref, bf16[64,1792]{1,0:T(8,128)(2,1)S(1)} %collective-permute-done.4.other_own_ref, ...), custom_call_target="tpu_custom_call" | custom-call | flops 134217728 | bytes 524288 | tf_op jit(solution)/shard_map/pallas_call | solution.py:304
  33.1 1.6 %collective-permute-start.9 = (bf16[256,256]{1,0:T(8,128)(2,1)S(1)}, bf16[256,256]{1,0:T(8,128)(2,1)S(1)}, u32[]{:S(2)}, u32[]{:S(2)}) collective-permute-start(bf16[256,256]{1,0:T(8,128)(2,1)S(1)} %get-tuple-element.37), channel_id=1, source_target_pairs={{0,2},{1,3},{2,0},{3,1},{4,6},{5,7},{6,4},{7,5},{8,10},{9,11},{10,... | collective-permute-start | bytes 393224 | tf_op jit(solution)/shard_map/ppermute | solution.py:23
  34.6 3.5 %collective-permute-done.9.got_ref = bf16[256,256]{1,0:T(8,128)(2,1)S(1)} collective-permute-done((bf16[256,256]{1,0:T(8,128)(2,1)S(1)}, bf16[256,256]{1,0:T(8,128)(2,1)S(1)}, u32[]{:S(2)}, u32[]{:S(2)}) %collective-permute-start.9) | collective-permute-done | bytes 131104 | tf_op jit(solution)/shard_map/ppermute | solution.py:23
  38.1 0.1 collective-permute-start.10
  38.2 1.5 %collective-permute-done.10.far_ref = f32[256,256]{1,0:T(8,128)S(1)} collective-permute-done((f32[256,256]{1,0:T(8,128)S(1)}, f32[256,256]{1,0:T(8,128)S(1)}, u32[]{:S(2)}, u32[]{:S(2)}) %collective-permute-start.10) | collective-permute-done | bytes 262176 | tf_op jit(solution)/shard_map/ppermute | solution.py:23
  39.7 2.1 %finish.1 = bf16[512,1024]{1,0:T(8,128)(2,1)} custom-call(s32[1]{0:T(128)} %bitcast.me_ref, f32[256,256]{1,0:T(8,128)S(1)} %shard_map.96.att_ref, f32[256,256]{1,0:T(8,128)S(1)} %collective-permute-done.10.far_ref, bf16[64,512]{1,0:T(8,128)(2,1)S(1)} %get-tuple-element.38.gate_own_ref, bf16[64,512]{1,0:T(8,128)(2,1)S(1)} %get-tuple-element.39.gate_far_ref, ...), custom_call_target="tpu_custom_call" | custom-call | flops 536870912 | bytes 1048576 | tf_op jit(solution)/shard_map/finish/pallas_call | solution.py:314
  (17 shorter events, 0.1 us)
Async XLA Ops:
  1.2 6.4 %collective-permute-start.1 = (bf16[4,2,64,256]{3,2,1,0:T(8,128)(2,1)S(1)}, bf16[4,2,64,256]{3,2,1,0:T(8,128)(2,1)S(1)}, u32[]{:S(2)}, u32[]{:S(2)}) collective-permute-start(bf16[4,2,64,256]{3,2,1,0:T(8,128)(2,1)S(1)} %get-tuple-element.24), channel_id=1, source_target_pairs={{0,1},{1,0},{2,3},{3,2},{4,5},{5,4},{6,7},{7,6},{8,9},{9,8},{10,11... | collective-permute-start | bytes 786440 | tf_op jit(solution)/shard_map/ppermute | solution.py:23
  1.7 5.8 %collective-permute-start = (bf16[16,1024]{1,0:T(8,128)(2,1)}, bf16[16,1024]{1,0:T(8,128)(2,1)S(1)}, u32[]{:S(2)}, u32[]{:S(2)}) collective-permute-start(bf16[16,1024]{1,0:T(8,128)(2,1)} %pool_ref.1), channel_id=1, source_target_pairs={{0,8},{1,9},{2,10},{3,11},{4,12},{5,13},{6,14},{7,15},{8,0},{9,1},... | collective-permute-start | bytes 98312 | tf_op jit(solution)/shard_map/ppermute | solution.py:23
  7.6 4.3 %collective-permute-start.2 = (bf16[32,1024]{1,0:T(8,128)(2,1)S(1)}, bf16[32,1024]{1,0:T(8,128)(2,1)S(1)}, u32[]{:S(2)}, u32[]{:S(2)}) collective-permute-start(bf16[32,1024]{1,0:T(8,128)(2,1)S(1)} %pad_maximum_fusion), channel_id=1, source_target_pairs={{0,4},{1,5},{2,6},{3,7},{4,0},{5,1},{6,2},{7,3},{8,12},{9,13},{10,... | collective-permute-start | bytes 196616 | tf_op jit(solution)/shard_map/ppermute | solution.py:23
  11.9 5.0 %collective-permute-start.3 = (bf16[64,1024]{1,0:T(8,128)(2,1)S(1)}, bf16[64,1024]{1,0:T(8,128)(2,1)S(1)}, u32[]{:S(2)}, u32[]{:S(2)}) collective-permute-start(bf16[64,1024]{1,0:T(8,128)(2,1)S(1)} %constant_dynamic-update-slice_fusion.rows_ref.own_ref), channel_id=1, source_target_pairs={{0,2},{1,3},{2,0},{3,1},{4,6},{5,7},{6,4},{7,5},{8,10},{9,11},{10,... | collective-permute-start | bytes 393224 | tf_op jit(solution)/shard_map/ppermute | solution.py:23
  13.7 1.6 %copy-start = (bf16[1024,1024]{1,0:T(8,128)(2,1)S(1)}, bf16[1024,1024]{1,0:T(8,128)(2,1)}, u32[]{:S(2)}) copy-start(bf16[1024,1024]{1,0:T(8,128)(2,1)} %w_ref.4) | copy-start | bytes 6291460
  15.3 1.6 %copy-start.1 = (bf16[1024,1024]{1,0:T(8,128)(2,1)S(1)}, bf16[1024,1024]{1,0:T(8,128)(2,1)}, u32[]{:S(2)}) copy-start(bf16[1024,1024]{1,0:T(8,128)(2,1)} %w_ref.4) | copy-start | bytes 6291460
  16.3 23.4 %copy-start.2 = (bf16[512,1024]{1,0:T(8,128)(2,1)S(1)}, bf16[512,1024]{1,0:T(8,128)(2,1)}, u32[]{:S(2)}) copy-start(bf16[512,1024]{1,0:T(8,128)(2,1)} %w_ref.5) | copy-start | bytes 3145732
  16.3 23.4 %copy-start.3 = (f32[512]{0:T(512)S(1)}, f32[512]{0:T(512)}, u32[]{:S(2)}) copy-start(f32[512]{0:T(512)} %param.13) | copy-start | bytes 6148
  16.3 16.1 %collective-permute-start.4 = (bf16[64,1792]{1,0:T(8,128)(2,1)S(1)}, bf16[64,1792]{1,0:T(8,128)(2,1)S(1)}, u32[]{:S(2)}, u32[]{:S(2)}) collective-permute-start(bf16[64,1792]{1,0:T(8,128)(2,1)S(1)} %get-tuple-element.28), channel_id=1, source_target_pairs={{0,1},{1,0},{2,3},{3,2},{4,5},{5,4},{6,7},{7,6},{8,9},{9,8},{10,11... | collective-permute-start | bytes 688136 | tf_op jit(solution)/shard_map/ppermute | solution.py:23
  17.4 15.0 %collective-permute-start.5 = (bf16[64,1792]{1,0:T(8,128)(2,1)S(1)}, bf16[64,1792]{1,0:T(8,128)(2,1)S(1)}, u32[]{:S(2)}, u32[]{:S(2)}) collective-permute-start(bf16[64,1792]{1,0:T(8,128)(2,1)S(1)} %get-tuple-element.29), channel_id=1, source_target_pairs={{0,1},{1,0},{2,3},{3,2},{4,5},{5,4},{6,7},{7,6},{8,9},{9,8},{10,11... | collective-permute-start | bytes 688136 | tf_op jit(solution)/shard_map/ppermute | solution.py:23
  17.5 6.0 %collective-permute-start.6 = (bf16[2,2,64,256]{3,2,1,0:T(8,128)(2,1)S(1)}, bf16[2,2,64,256]{3,2,1,0:T(8,128)(2,1)S(1)}, u32[]{:S(2)}, u32[]{:S(2)}) collective-permute-start(bf16[2,2,64,256]{3,2,1,0:T(8,128)(2,1)S(1)} %get-tuple-element.33), channel_id=1, source_target_pairs={{0,4},{1,5},{2,6},{3,7},{4,0},{5,1},{6,2},{7,3},{8,12},{9,13},{10,... | collective-permute-start | bytes 393224 | tf_op jit(solution)/shard_map/ppermute | solution.py:23
  19.4 13.0 %collective-permute-start.7 = (bf16[2,2,64,256]{3,2,1,0:T(8,128)(2,1)S(1)}, bf16[2,2,64,256]{3,2,1,0:T(8,128)(2,1)S(1)}, u32[]{:S(2)}, u32[]{:S(2)}) collective-permute-start(bf16[2,2,64,256]{3,2,1,0:T(8,128)(2,1)S(1)} %get-tuple-element.34), channel_id=1, source_target_pairs={{0,8},{1,9},{2,10},{3,11},{4,12},{5,13},{6,14},{7,15},{8,0},{9,1},... | collective-permute-start | bytes 393224 | tf_op jit(solution)/shard_map/ppermute | solution.py:23
  22.4 10.0 %collective-permute-start.8 = (bf16[2,2,64,256]{3,2,1,0:T(8,128)(2,1)S(1)}, bf16[2,2,64,256]{3,2,1,0:T(8,128)(2,1)S(1)}, u32[]{:S(2)}, u32[]{:S(2)}) collective-permute-start(bf16[2,2,64,256]{3,2,1,0:T(8,128)(2,1)S(1)} %get-tuple-element.35), channel_id=1, source_target_pairs={{0,12},{1,13},{2,14},{3,15},{4,8},{5,9},{6,10},{7,11},{8,4},{9,5},... | collective-permute-start | bytes 393224 | tf_op jit(solution)/shard_map/ppermute | solution.py:23
  33.1 5.0 %collective-permute-start.9 = (bf16[256,256]{1,0:T(8,128)(2,1)S(1)}, bf16[256,256]{1,0:T(8,128)(2,1)S(1)}, u32[]{:S(2)}, u32[]{:S(2)}) collective-permute-start(bf16[256,256]{1,0:T(8,128)(2,1)S(1)} %get-tuple-element.37), channel_id=1, source_target_pairs={{0,2},{1,3},{2,0},{3,1},{4,6},{5,7},{6,4},{7,5},{8,10},{9,11},{10,... | collective-permute-start | bytes 393224 | tf_op jit(solution)/shard_map/ppermute | solution.py:23
  38.1 1.6 %collective-permute-start.10 = (f32[256,256]{1,0:T(8,128)S(1)}, f32[256,256]{1,0:T(8,128)S(1)}, u32[]{:S(2)}, u32[]{:S(2)}) collective-permute-start(f32[256,256]{1,0:T(8,128)S(1)} %shard_map.96.att_ref), channel_id=1, source_target_pairs={{0,1},{1,0},{2,3},{3,2},{4,5},{5,4},{6,7},{7,6},{8,9},{9,8},{10,11... | collective-permute-start | bytes 786440 | tf_op jit(solution)/shard_map/ppermute | solution.py:23
